TPU v7x, 128 devices: a whole 4x4x4 slice. The times are simulated.
128 devices in a mesh: row: 8 (over x, z_lo), col: 16 (over y, z_hi, core).
Axes of the slice: x: 4, y: 4, z: 4 (z_hi: 2, z_lo: 2; z = z_hi * 2 + z_lo), core: 2. Of those that a mesh axis runs over, the one named last changes fastest.
Arguments:
- momentum: bfloat16 [16384, 16384], P('row', 'col'), may hold values from -6 to 6
- gradient: bfloat16 [16384, 16384], P('row', 'col'), may hold values from -43 to 43
- right_prev: float32 [16384, 512], P('col'), may hold values from -6 to 6
- weight: bfloat16 [16384, 16384], P('col', 'row'), may hold values from -0.046875 to 0.046875
- tokens: bfloat16 [256, 16384], P(None, 'row'), may hold values from -6 to 6
Outputs:
- new_momentum: bfloat16 [16384, 16384], P('row', 'col')
- new_basis: float32 [16384, 512], P('col')
- new_weight: bfloat16 [16384, 16384], P('col', 'row')
- projected: bfloat16 [256, 16384], P('row', 'col')
All inputs are finite; a program needn't handle non-finite values.
Results may differ from a plain program's by a relative error of at most 0.006.
Values may be sent and summed in bfloat16 or wider, within the bound.
No kernel may reach another device: no remote copies, remote signals or barrier semaphores. Data moves between devices by JAX's collectives and lax.ppermute only.
A program may use at most 128 MiB of HBM per device.

v0:
```python
import functools
import jax
import jax.numpy as jnp
from jax import lax
from jax.sharding import Mesh
from jax.sharding import PartitionSpec as P

DIN = 16384
COL = ("col_0", "col_1", "col_2")
ROW = ("row_0", "row_1")
ROW_COL = ("row_0", "row_1", "col_0", "col_1", "col_2")
decay_part = 0.05
step_size = 0.01
epsilon = 1e-06


def cut_along(array, dim, length):
    shape = array.shape
    pieces = array.reshape(*shape[:dim], length, shape[dim] // length, *shape[dim + 1 :])
    return jnp.moveaxis(pieces, dim, 0)


def summed_on_arrival(array, axis, dim):
    length = lax.axis_size(axis)
    pieces = lax.all_to_all(cut_along(array, dim, length), axis, 0, 0, tiled=True)
    return jnp.sum(pieces, axis=0)


def over_axes(array, axes):
    return functools.reduce(lax.psum, axes, array)


def joined_along(pieces, dim):
    pieces = jnp.moveaxis(pieces, 0, dim)
    shape = pieces.shape
    return pieces.reshape(*shape[:dim], shape[dim] * shape[dim + 1], *shape[dim + 2 :])


def from_everyone(array, axis):
    length = lax.axis_size(axis)
    return lax.all_to_all(
        jnp.broadcast_to(array[None], (length, *array.shape)), axis, 0, 0, tiled=True
    )


def collect(array, axis, dim):
    return joined_along(from_everyone(array, axis), dim)


def filled_up(lines, length):
    spare = -len(lines) % length
    return jnp.pad(lines, [(0, spare)] + [(0, 0)] * (lines.ndim - 1))


def spread(array, axis, root):
    lines = jnp.where(lax.axis_index(axis) == root, array, jnp.zeros_like(array)).reshape(
        -1, *array.shape[1:][-1:]
    )
    padded = filled_up(lines, lax.axis_size(axis))
    own = lax.psum_scatter(padded, axis, scatter_dimension=0, tiled=True)
    return lax.all_gather(own, axis, axis=0, tiled=True)[: len(lines)].reshape(array.shape)


def from_root(array, axis, root):
    return lax.dynamic_index_in_dim(lax.all_gather(array, axis), root, 0, keepdims=False)


def contract_first(lhs, rhs, highest):
    return lax.dot_general(
        lhs, rhs, (((0,), (0,)), ((), ())), precision=highest, preferred_element_type=jnp.float32
    )


def contract_last(lhs, rhs, highest):
    return lax.dot_general(
        lhs, rhs, (((1,), (1,)), ((), ())), precision=highest, preferred_element_type=jnp.float32
    )


def per_device(momentum, gradient, right_prev, weight, tokens):
    highest = lax.Precision.HIGHEST
    mixed = momentum.astype(jnp.float32) + gradient.astype(jnp.float32)
    partial_left = jnp.dot(mixed, right_prev, precision=highest, preferred_element_type=jnp.float32)
    left_raw = lax.psum(partial_left, COL)
    gram_matrix = lax.psum(contract_first(left_raw, left_raw, highest), ROW)
    factor = jnp.linalg.cholesky(gram_matrix)
    left_factor = lax.linalg.triangular_solve(
        factor, left_raw, left_side=False, lower=True, transpose_a=True
    )
    partial_right = contract_first(mixed, left_factor, highest)
    right_shard = summed_on_arrival(partial_right, ROW, 0)
    squares = over_axes(jnp.sum(right_shard * right_shard, axis=0), ROW_COL)
    right_factor = collect(right_shard, ROW, 0)
    new_basis = right_factor * lax.rsqrt(squares / DIN + epsilon)
    outer = contract_last(left_factor, right_factor, highest)
    new_momentum = (mixed - decay_part * outer).astype(jnp.bfloat16)
    span_count = lax.axis_size(COL) // lax.axis_size(ROW)
    col_index = lax.axis_index(COL)
    row_index = lax.axis_index(ROW)
    block_rows = left_factor.shape[0] // span_count
    own_block = lax.dynamic_slice_in_dim(
        left_factor, col_index % span_count * block_rows, block_rows, 0
    )
    left_tile = spread(own_block.astype(jnp.bfloat16), ROW, col_index // span_count)
    basis_send = new_basis.astype(jnp.bfloat16)
    pieces = [
        from_root(basis_send, COL, row_index * span_count + piece_index)
        for piece_index in range(span_count)
    ]
    basis_tile = jnp.concatenate(pieces, axis=0)
    update = lax.dot_general(
        left_tile, basis_tile, (((1,), (1,)), ((), ())), preferred_element_type=jnp.float32
    )
    new_weight = (weight.astype(jnp.float32) - step_size * update).astype(jnp.bfloat16)
    projected = summed_on_arrival(
        lax.dot_general(
            tokens, new_weight, (((1,), (1,)), ((), ())), preferred_element_type=jnp.float32
        ),
        ROW,
        0,
    ).astype(jnp.bfloat16)
    return (new_momentum, new_basis, new_weight, projected)


def solution(mesh):
    torus = Mesh(mesh.devices.reshape(4, 2, 4, 2, 2), ("row_0", "row_1", "col_0", "col_1", "col_2"))
    placed = (P(ROW, COL), P(ROW, COL), P(COL, None), P(COL, ROW), P(None, ROW))
    return jax.shard_map(
        per_device,
        mesh=torus,
        in_specs=placed,
        out_specs=(P(ROW, COL), P(COL, None), P(COL, ROW), P(ROW, COL)),
        check_vma=False,
    )
```

profile of v0, /device:TPU:10, one launch (start us, length us, event | category | flops | bytes accessed | tf_op | source)
XLA Modules:
  0.0 747.0 jit_solution(4212846563401317149)
XLA Ops:
  7.2 1.5 copy-done
  8.8 17.3 %fusion.1 = f32[2048,512]{1,0:T(8,128)} fusion(f32[1024,512]{1,0:T(8,128)S(1)} %copy-done, bf16[2048,1024]{1,0:T(8,128)(2,1)} %param.6, bf16[2048,1024]{1,0:T(8,128)(2,1)} %param.5), kind=kOutput, calls=%fused_computation.6 | convolution fusion | flops 12891193344 | bytes 14680064 | tf_op jit(solution)/shard_map/dot_general | solution.py:83
  26.2 147.3 %all-reduce.4.cloned.1.call-done = f32[2048,512]{1,0:T(8,128)} async-done(((f32[2048,512]{1,0:T(8,128)}), f32[2048,512]{1,0:T(8,128)}) %all-reduce.4.cloned.1.call-update) | async-done | bytes 4194320 | tf_op jit(solution)/shard_map/psum | solution.py:84
  173.5 11.6 %fusion.43 = f32[512,512]{0,1:T(8,128)} fusion(f32[2048,512]{1,0:T(8,128)} %all-reduce.4.cloned.1.call-done), kind=kOutput, calls=%fused_computation.86 | convolution fusion | flops 6442450944 | bytes 5242880 | tf_op jit(solution)/shard_map/dot_general | solution.py:69
  185.1 83.7 %all-reduce.6.cloned.1.call-done = f32[512,512]{0,1:T(8,128)} async-done(((f32[512,512]{0,1:T(8,128)}), f32[512,512]{0,1:T(8,128)}) %all-reduce.6.cloned.1.call-update) | async-done | bytes 1048592 | tf_op jit(solution)/shard_map/psum | solution.py:85
  268.8 1.6 copy.12
  270.4 1.4 fusion.21
  271.9 11.7 %cholesky.104 = f32[128,128]{1,0:T(8,128)S(1)} custom-call(f32[128,128]{1,0:T(8,128)S(1)} %cholesky.266), custom_call_target="Cholesky" | custom-call | tf_op jit(solution)/shard_map/jit(cholesky)/cholesky | solution.py:86
  283.6 9.8 %custom-call.30 = f32[1,128,128]{1,2,0:T(8,128)S(1)} custom-call(f32[1,128,128]{2,1,0:T(8,128)S(1)} %get-tuple-element.33), custom_call_target="InvertDiagBlocksLowerTriangular" | custom-call | tf_op jit(solution)/shard_map/jit(cholesky)/cholesky | solution.py:86
  293.6 0.3 constant_dynamic-update-slice_fusion.1
  293.9 0.3 convolution_subtract_fusion.2
  294.2 11.7 %cholesky.217 = f32[128,128]{1,0:T(8,128)S(1)} custom-call(f32[128,128]{1,0:T(8,128)S(1)} %cholesky.270), custom_call_target="Cholesky" | custom-call | tf_op jit(solution)/shard_map/jit(cholesky)/cholesky | solution.py:86
  306.0 10.2 %custom-call.31 = f32[1,128,128]{1,2,0:T(8,128)S(1)} custom-call(f32[1,128,128]{2,1,0:T(8,128)S(1)} %get-tuple-element.30), custom_call_target="InvertDiagBlocksLowerTriangular" | custom-call | tf_op jit(solution)/shard_map/jit(cholesky)/cholesky | solution.py:86
  316.4 0.4 convolution_subtract_fusion.3
  316.8 11.7 %cholesky.238 = f32[128,128]{1,0:T(8,128)S(1)} custom-call(f32[128,128]{1,0:T(8,128)S(1)} %cholesky.275), custom_call_target="Cholesky" | custom-call | tf_op jit(solution)/shard_map/jit(cholesky)/cholesky | solution.py:86
  328.6 0.6 compare_reduce_fusion.1
  329.2 9.8 %custom-call.32 = f32[1,128,128]{1,2,0:T(8,128)S(1)} custom-call(f32[1,128,128]{2,1,0:T(8,128)S(1)} %get-tuple-element.27), custom_call_target="InvertDiagBlocksLowerTriangular" | custom-call | tf_op jit(solution)/shard_map/jit(cholesky)/cholesky | solution.py:86
  339.3 0.4 convolution_subtract_fusion.4
  339.6 11.7 %cholesky.255 = f32[128,128]{1,0:T(8,128)S(1)} custom-call(f32[128,128]{1,0:T(8,128)S(1)} %convolution_subtract_fusion.4), custom_call_target="Cholesky" | custom-call | tf_op jit(solution)/shard_map/jit(cholesky)/cholesky | solution.py:86
  351.4 0.7 compare_reduce_fusion
  352.0 0.6 compare_reduce_fusion.2
  355.2 0.3 select_select_fusion
  355.6 8.0 %while.1 = (s32[]{:T(128)}, f32[512,512]{1,0:T(8,128)S(1)}, s32[4,2]{0,1:T(2,128)S(1)}, f32[4,128,128]{2,1,0:T(8,128)S(1)}, s32[]{:T(128)}) while((s32[]{:T(128)}, f32[512,512]{1,0:T(8,128)S(1)}, s32[4,2]{0,1:T(2,128)S(1)}, f32[4,128,128]{2,1,0:T(8,128)S(1)}, s32[]{:T(128)}) %tuple.32), condition=%wide.while_cond, body=%wide.while_body.sunk | while | flops 2 | bytes 131189 | solution.py:87
  355.7 0.5 fusion.58
  356.2 1.4 bitcast_dynamic-update-slice_fusion.2
  357.7 0.5 fusion.58
  358.2 1.4 bitcast_dynamic-update-slice_fusion.2
  359.7 0.5 fusion.58
  360.2 1.4 bitcast_dynamic-update-slice_fusion.2
  361.7 0.5 fusion.58
  362.2 1.4 bitcast_dynamic-update-slice_fusion.2
  363.6 39.3 %custom-call.33 = f32[4,128,128]{1,2,0:T(8,128)S(1)} custom-call(f32[4,128,128]{2,1,0:T(8,128)S(1)} %get-tuple-element.11), custom_call_target="InvertDiagBlocksLowerTriangular" | custom-call | tf_op jit(solution)/shard_map/triangular_solve | solution.py:87
  402.9 2.5 fusion.19
  405.4 3.1 convolution_subtract_fusion.1
  408.5 1.1 fusion.32
  409.6 4.6 convolution_subtract_fusion
  414.2 1.1 fusion.31
  415.3 7.2 fusion.8
  422.6 1.1 fusion.30
  423.7 27.9 %fusion = f32[1024,512]{1,0:T(8,128)} fusion(bf16[2048,1024]{1,0:T(8,128)(2,1)S(1)} %copy-done.8, bf16[2048,1024]{1,0:T(8,128)(2,1)S(1)} %copy-done.9, f32[2048,128]{0,1:T(8,128)S(1)} %fusion.30, f32[2048,128]{0,1:T(8,128)S(1)} %fusion.31, f32[2048,128]{0,1:T(8,128)S(1)} %fusion.32, f32[2048,128]{0,1:T(8,128)S(1)} %fusion.19), kind=kOutput, calls=%fused_computation.5 | convolution fusion | flops 12894339072 | bytes 14680064 | tf_op jit(solution)/shard_map/dot_general | solution.py:69
  451.6 6.2 all-to-all-start
  457.8 2.9 pad_maximum_fusion
  460.7 20.1 %all-to-all-done = f32[8,128,512]{2,1,0:T(8,128)} async-done(((f32[8,128,512]{2,1,0:T(8,128)}), f32[8,128,512]{2,1,0:T(8,128)}, u32[]{:S(2)}, u32[]{:S(2)}) %all-to-all-start) | async-done | bytes 2097184 | tf_op jit(solution)/shard_map/all_to_all | solution.py:25
  480.7 1.8 reduce_sum.27
  482.6 1.6 broadcast_in_dim.6
  484.1 5.7 all-to-all-start.1
  489.9 2.4 fusion.18
  492.3 2.3 copy.14
  494.7 21.2 %psum.51 = f32[512]{0:T(512)S(1)} all-reduce(f32[512]{0:T(512)S(1)} %multiply_reduce_fusion), channel_id=1, replica_groups=mesh['row_0'=4,'row_1'=2,'col_0'=4,'col_1'=2,'col_2'=2] {'row_0'}, use_global_device_ids=true, to_apply=%region_12.13 | all-reduce | flops 512 | bytes 4096 | tf_op jit(solution)/shard_map/psum | solution.py:30
  515.9 5.4 psum.52
  521.3 8.6 %psum.53 = f32[512]{0:T(512)S(1)} all-reduce(f32[512]{0:T(512)S(1)} %psum.52), channel_id=1, replica_groups=mesh['row_0'=4,'row_1'=2,'col_0'=4,'col_1'=2,'col_2'=2] {'col_0'}, use_global_device_ids=true, to_apply=%region_14.15 | all-reduce | flops 512 | bytes 4096 | tf_op jit(solution)/shard_map/psum | solution.py:30
  529.8 6.6 psum.54
  536.4 2.4 psum.55
  538.9 1.4 fusion.17
  540.4 1.7 copy.15
  542.1 1.6 broadcast_multiply_fusion
  543.7 106.3 %all-gather.5.cloned.1.call-done = bf16[16,1024,512]{2,1,0:T(8,128)(2,1)} async-done(((bf16[1,1024,512]{2,1,0:T(8,128)(2,1)}), bf16[16,1024,512]{2,1,0:T(8,128)(2,1)}) %all-gather.5.cloned.1.call-update) | async-done | bytes 16777232 | tf_op jit(solution)/shard_map/all_gather | solution.py:65
  649.9 1.7 dynamic-slice_bitcast_fusion.1
  651.6 39.3 %all-gather.3.cloned.1.call-done = bf16[1024,512]{0,1:T(8,128)(2,1)} async-done(((bf16[128,512]{0,1:T(8,128)(2,1)}), bf16[1024,512]{0,1:T(8,128)(2,1)}) %all-gather.3.cloned.1.call-update) | async-done | bytes 1048592 | tf_op jit(solution)/shard_map/all_gather | solution.py:61
  691.0 5.0 subtract_convert_fusion
  696.0 2.4 fusion.44
  698.4 8.6 %all-to-all-start.2 = ((f32[8,32,1024]{2,1,0:T(8,128)}), f32[8,32,1024]{2,1,0:T(8,128)}, u32[]{:S(2)}, u32[]{:S(2)}) async-start(f32[8,32,1024]{2,1,0:T(8,128)} %bitcast.17), calls=%async_computation.2 | async-start | bytes 2097152 | tf_op jit(solution)/shard_map/all_to_all | solution.py:25
  707.0 31.3 %subtract_convert_fusion.1 = bf16[2048,1024]{1,0:T(8,128)(2,1)} fusion(bf16[2048,1024]{1,0:T(8,128)(2,1)} %param.6, bf16[2048,1024]{1,0:T(8,128)(2,1)} %param.5, f32[1024,512]{1,0:T(8,128)} %bitcast.72, f32[2048,128]{0,1:T(8,128)} %copy-done.6, f32[2048,128]{0,1:T(8,128)} %copy-done.5, f32[2048,128]{0,1:T(8,128)} %copy-done.4, f32[2048,128]{0,1:T(8,128)S(1)} %fusion.19), kind=kOutput, calls=%fused_computation.3 | convolution fusion | flops 12900630528 | bytes 18874368 | tf_op jit(solution)/shard_map/dot_general | solution.py:75
  738.3 1.9 reduce_sum.29
  (55 shorter events, 1.4 us)
Async XLA Ops:
  7.2 1.6 copy-start
  7.2 166.3 %all-reduce.4.cloned.1.call-start = ((), (), s32[]{:S(2)}) async-start(), calls=%async_computation.4 | async-start | bytes 8388608 | tf_op jit(solution)/shard_map/psum | solution.py:84
  26.1 242.7 %all-reduce.6.cloned.1.call-start = ((), (), s32[]{:S(2)}) async-start(), calls=%async_computation.5 | async-start | bytes 2097152 | tf_op jit(solution)/shard_map/psum | solution.py:85
  363.6 39.3 %copy-start.7 = (f32[512,512]{1,0:T(8,128)}, f32[512,512]{1,0:T(8,128)S(1)}, u32[]{:S(2)}) copy-start(f32[512,512]{1,0:T(8,128)S(1)} %get-tuple-element.100) | copy-start | bytes 3145732
  402.9 6.6 copy-start.2
  409.6 48.2 %copy-start.4 = (f32[2048,128]{0,1:T(8,128)}, f32[2048,128]{0,1:T(8,128)S(1)}, u32[]{:S(2)}) copy-start(f32[2048,128]{0,1:T(8,128)S(1)} %fusion.32) | copy-start | bytes 3145732
  414.2 9.5 %copy-start.9 = (bf16[2048,1024]{1,0:T(8,128)(2,1)S(1)}, bf16[2048,1024]{1,0:T(8,128)(2,1)}, u32[]{:S(2)}) copy-start(bf16[2048,1024]{1,0:T(8,128)(2,1)} %param.5) | copy-start | bytes 12582916
  415.3 42.5 %copy-start.5 = (f32[2048,128]{0,1:T(8,128)}, f32[2048,128]{0,1:T(8,128)S(1)}, u32[]{:S(2)}) copy-start(f32[2048,128]{0,1:T(8,128)S(1)} %fusion.31) | copy-start | bytes 3145732
  415.3 8.4 %copy-start.8 = (bf16[2048,1024]{1,0:T(8,128)(2,1)S(1)}, bf16[2048,1024]{1,0:T(8,128)(2,1)}, u32[]{:S(2)}) copy-start(bf16[2048,1024]{1,0:T(8,128)(2,1)} %param.6) | copy-start | bytes 12582916
  423.7 27.9 %copy-start.6 = (f32[2048,128]{0,1:T(8,128)}, f32[2048,128]{0,1:T(8,128)S(1)}, u32[]{:S(2)}) copy-start(f32[2048,128]{0,1:T(8,128)S(1)} %fusion.30) | copy-start | bytes 3145732
  451.6 29.1 %all-to-all-start = ((f32[8,128,512]{2,1,0:T(8,128)}), f32[8,128,512]{2,1,0:T(8,128)}, u32[]{:S(2)}, u32[]{:S(2)}) async-start(f32[8,128,512]{2,1,0:T(8,128)} %bitcast.73), calls=%async_computation | async-start | bytes 4194304 | tf_op jit(solution)/shard_map/all_to_all | solution.py:25
  484.1 54.7 %all-to-all-start.1 = ((f32[8,128,512]{2,1,0:T(8,128)}), f32[8,128,512]{2,1,0:T(8,128)S(1)}, u32[]{:S(2)}, u32[]{:S(2)}) async-start(f32[8,128,512]{2,1,0:T(8,128)} %broadcast_in_dim.6), calls=%async_computation.1 | async-start | bytes 4194304 | tf_op jit(solution)/shard_map/all_to_all | solution.py:41
  489.9 50.5 %reduce-scatter.4.cloned.1.call-start = ((), (), s32[]{:S(2)}) async-start(), calls=%async_computation.8 | async-start | bytes 1179648
  494.6 155.3 %all-gather.5.cloned.1.call-start = ((), (), s32[]{:S(2)}) async-start(), calls=%async_computation.7 | async-start | bytes 17825792 | tf_op jit(solution)/shard_map/all_gather | solution.py:65
  538.9 4.8 copy-start.3
  540.3 150.7 %all-gather.3.cloned.1.call-start = ((), (), s32[]{:S(2)}) async-start(), calls=%async_computation.6 | async-start | bytes 1179648 | tf_op jit(solution)/shard_map/all_gather | solution.py:61
  691.0 5.0 copy-start.10
  696.0 2.4 copy-start.11
  698.4 39.9 %all-to-all-start.2 = ((f32[8,32,1024]{2,1,0:T(8,128)}), f32[8,32,1024]{2,1,0:T(8,128)}, u32[]{:S(2)}, u32[]{:S(2)}) async-start(f32[8,32,1024]{2,1,0:T(8,128)} %bitcast.17), calls=%async_computation.2 | async-start | bytes 2097152 | tf_op jit(solution)/shard_map/all_to_all | solution.py:25
  707.0 33.3 %copy-start.1 = (f32[1024,512]{1,0:T(8,128)S(1)}, f32[1024,512]{1,0:T(8,128)}, u32[]{:S(2)}) copy-start(f32[1024,512]{1,0:T(8,128)} %param.7) | copy-start | bytes 6291460
Sparse Core Ops, SparseCore 0:
  26.2 147.1 all-reduce.3
  185.2 83.6 all-reduce.5
  494.7 43.9 reduce-scatter.3
  541.5 108.3 all-gather.4
  651.9 38.9 all-gather.2
where the time goes:
time: 755 us; the launch traced here: 747 us
  waiting for transfers between devices  397 us (53%)
  other arithmetic  132 us (17%)
  matrix products  118 us (16%)
  blocking collectives  44.2 us (6%)
  starting transfers between devices  20.7 us (3%)
  local copies, waits for them, and re-layouts  18.4 us (2%)
  between operations  16.9 us (2%)
    psum x1, waiting for transfers between devices, per_device(): left_raw = lax.psum(partial_left, COL)  147 us
    all_gather x1, waiting for transfers between devices, from_root(): lax.all_gather(array, axis)  106 us
    psum x1, waiting for transfers between devices, per_device(): gram_matrix = lax.psum(contract_first(left_raw, left_raw, highest), ROW)  83.7 us
    another operation x14, other arithmetic, per_device(): factor = jnp.linalg.cholesky(gram_matrix)  78.7 us
    psum x5, blocking collectives, over_axes(): return functools.reduce(lax.psum, axes, array)  44.2 us
    another operation x4, other arithmetic, per_device(): lax.linalg.triangular_solve(factor, left_raw, left_side=False, lower=True...  42.5 us
    dot_general x2, matrix products, contract_first(): lax.dot_general(lhs, rhs, (((0,), (0,)), ((), ())), precision=highest, pr...  39.5 us
    all_gather x1, waiting for transfers between devices, spread(): lax.all_gather(own, axis, axis=0, tiled=True)[:len(lines)]  39.3 us
  transfers between devices with their start and end apart: 8, of which 5 were waited for; matrix products, arithmetic and copies ran while one was open for 6% of the time, Pallas kernels for 0%

commit v1 on v0

--- a/solution.py
+++ b/solution.py
@@ -78,10 +78,14 @@
 
 
 def per_device(momentum, gradient, right_prev, weight, tokens):
+
+    def open_zones_on(in_array):
+        return jax.lax.psum(jax.lax.psum(in_array, "col_0"), ("col_1", "col_2"))
+
     highest = lax.Precision.HIGHEST
     mixed = momentum.astype(jnp.float32) + gradient.astype(jnp.float32)
     partial_left = jnp.dot(mixed, right_prev, precision=highest, preferred_element_type=jnp.float32)
-    left_raw = lax.psum(partial_left, COL)
+    left_raw = open_zones_on(partial_left)
     gram_matrix = lax.psum(contract_first(left_raw, left_raw, highest), ROW)
     factor = jnp.linalg.cholesky(gram_matrix)
     left_factor = lax.linalg.triangular_solve(

time: 755 us -> 791 us (1.048)
  waiting for transfers between devices: 397 us -> 433 us
    psum x1 -> x2, waiting for transfers between devices: 147 us -> 191 us  [open_zones_on(): return jax.lax.psum(jax.lax.psum(in_array, 'col_0'), ('col_1', 'col_2'))]
  transfers between devices with their start and end apart: 8 -> 9, of which waited for: 5 -> 6; matrix products, arithmetic and copies ran while one was open for 6% -> 6% of each run, Pallas kernels for 0% -> 0%
where the time goes in v1:
time: 791 us; the launch traced here: 783 us
  waiting for transfers between devices  433 us (55%)
  other arithmetic  132 us (17%)
  matrix products  118 us (15%)
  blocking collectives  44.1 us (6%)
  starting transfers between devices  20.7 us (3%)
  local copies, waits for them, and re-layouts  18.4 us (2%)
  between operations  17.2 us (2%)
    psum x2, waiting for transfers between devices, open_zones_on(): return jax.lax.psum(jax.lax.psum(in_array, 'col_0'), ('col_1', 'col_2'))  191 us
    all_gather x1, waiting for transfers between devices, from_root(): lax.all_gather(array, axis)  106 us
    another operation x14, other arithmetic, per_device(): factor = jnp.linalg.cholesky(gram_matrix)  78.7 us
    psum x1, waiting for transfers between devices, per_device(): gram_matrix = lax.psum(contract_first(left_raw, left_raw, highest), ROW)  75.9 us
    psum x5, blocking collectives, over_axes(): return functools.reduce(lax.psum, axes, array)  44.1 us
    another operation x4, other arithmetic, per_device(): lax.linalg.triangular_solve(factor, left_raw, left_side=False, lower=True...  42.5 us
    dot_general x2, matrix products, contract_first(): lax.dot_general(lhs, rhs, (((0,), (0,)), ((), ())), precision=highest, pr...  39.5 us
    all_gather x1, waiting for transfers between devices, spread(): lax.all_gather(own, axis, axis=0, tiled=True)[:len(lines)]  39.4 us
  transfers between devices with their start and end apart: 9, of which 6 were waited for; matrix products, arithmetic and copies ran while one was open for 6% of the time, Pallas kernels for 0%

profile of v1, /device:TPU:10, one launch (start us, length us, event | category | flops | bytes accessed | tf_op | source)
XLA Modules:
  0.0 783.0 jit_solution(7679584187423759304)
XLA Ops:
  7.2 1.5 copy-done
  8.8 17.3 %fusion.1 = f32[2048,512]{1,0:T(8,128)} fusion(f32[1024,512]{1,0:T(8,128)S(1)} %copy-done, bf16[2048,1024]{1,0:T(8,128)(2,1)} %param.6, bf16[2048,1024]{1,0:T(8,128)(2,1)} %param.5), kind=kOutput, calls=%fused_computation.6 | convolution fusion | flops 12891193344 | bytes 14680064 | tf_op jit(solution)/shard_map/dot_general | solution.py:87
  26.2 94.0 %all-reduce.5.cloned.1.call-done = f32[2048,512]{1,0:T(8,128)} async-done(((f32[2048,512]{1,0:T(8,128)}), f32[2048,512]{1,0:T(8,128)}) %all-reduce.5.cloned.1.call-update) | async-done | bytes 4194320 | tf_op jit(solution)/shard_map/psum | solution.py:83
  120.3 96.6 %all-reduce.7.cloned.1.call-done = f32[2048,512]{1,0:T(8,128)} async-done(((f32[2048,512]{1,0:T(8,128)}), f32[2048,512]{1,0:T(8,128)}) %all-reduce.7.cloned.1.call-update) | async-done | bytes 4194320 | tf_op jit(solution)/shard_map/psum | solution.py:83
  216.9 11.6 %fusion.43 = f32[512,512]{0,1:T(8,128)} fusion(f32[2048,512]{1,0:T(8,128)} %all-reduce.7.cloned.1.call-done), kind=kOutput, calls=%fused_computation.86 | convolution fusion | flops 6442450944 | bytes 5242880 | tf_op jit(solution)/shard_map/dot_general | solution.py:69
  228.5 75.9 %all-reduce.9.cloned.1.call-done = f32[512,512]{0,1:T(8,128)} async-done(((f32[512,512]{0,1:T(8,128)}), f32[512,512]{0,1:T(8,128)}) %all-reduce.9.cloned.1.call-update) | async-done | bytes 1048592 | tf_op jit(solution)/shard_map/psum | solution.py:89
  304.4 1.6 copy.12
  306.0 1.4 fusion.21
  307.5 11.7 %cholesky.104 = f32[128,128]{1,0:T(8,128)S(1)} custom-call(f32[128,128]{1,0:T(8,128)S(1)} %cholesky.266), custom_call_target="Cholesky" | custom-call | tf_op jit(solution)/shard_map/jit(cholesky)/cholesky | solution.py:90
  319.2 9.8 %custom-call.30 = f32[1,128,128]{1,2,0:T(8,128)S(1)} custom-call(f32[1,128,128]{2,1,0:T(8,128)S(1)} %get-tuple-element.33), custom_call_target="InvertDiagBlocksLowerTriangular" | custom-call | tf_op jit(solution)/shard_map/jit(cholesky)/cholesky | solution.py:90
  329.2 0.3 constant_dynamic-update-slice_fusion.1
  329.5 0.3 convolution_subtract_fusion.2
  329.8 11.7 %cholesky.217 = f32[128,128]{1,0:T(8,128)S(1)} custom-call(f32[128,128]{1,0:T(8,128)S(1)} %cholesky.270), custom_call_target="Cholesky" | custom-call | tf_op jit(solution)/shard_map/jit(cholesky)/cholesky | solution.py:90
  341.6 10.2 %custom-call.31 = f32[1,128,128]{1,2,0:T(8,128)S(1)} custom-call(f32[1,128,128]{2,1,0:T(8,128)S(1)} %get-tuple-element.30), custom_call_target="InvertDiagBlocksLowerTriangular" | custom-call | tf_op jit(solution)/shard_map/jit(cholesky)/cholesky | solution.py:90
  352.0 0.4 convolution_subtract_fusion.3
  352.4 11.7 %cholesky.238 = f32[128,128]{1,0:T(8,128)S(1)} custom-call(f32[128,128]{1,0:T(8,128)S(1)} %cholesky.275), custom_call_target="Cholesky" | custom-call | tf_op jit(solution)/shard_map/jit(cholesky)/cholesky | solution.py:90
  364.2 0.6 compare_reduce_fusion.1
  364.8 9.8 %custom-call.32 = f32[1,128,128]{1,2,0:T(8,128)S(1)} custom-call(f32[1,128,128]{2,1,0:T(8,128)S(1)} %get-tuple-element.27), custom_call_target="InvertDiagBlocksLowerTriangular" | custom-call | tf_op jit(solution)/shard_map/jit(cholesky)/cholesky | solution.py:90
  374.9 0.4 convolution_subtract_fusion.4
  375.2 11.7 %cholesky.255 = f32[128,128]{1,0:T(8,128)S(1)} custom-call(f32[128,128]{1,0:T(8,128)S(1)} %convolution_subtract_fusion.4), custom_call_target="Cholesky" | custom-call | tf_op jit(solution)/shard_map/jit(cholesky)/cholesky | solution.py:90
  387.0 0.7 compare_reduce_fusion
  387.6 0.6 compare_reduce_fusion.2
  391.2 8.0 %while.1 = (s32[]{:T(128)}, f32[512,512]{1,0:T(8,128)S(1)}, s32[4,2]{0,1:T(2,128)S(1)}, f32[4,128,128]{2,1,0:T(8,128)S(1)}, s32[]{:T(128)}) while((s32[]{:T(128)}, f32[512,512]{1,0:T(8,128)S(1)}, s32[4,2]{0,1:T(2,128)S(1)}, f32[4,128,128]{2,1,0:T(8,128)S(1)}, s32[]{:T(128)}) %tuple.32), condition=%wide.while_cond, body=%wide.while_body.sunk | while | flops 2 | bytes 131189 | solution.py:91
  391.3 0.5 fusion.58
  391.8 1.4 bitcast_dynamic-update-slice_fusion.2
  393.3 0.5 fusion.58
  393.8 1.4 bitcast_dynamic-update-slice_fusion.2
  395.3 0.5 fusion.58
  395.8 1.4 bitcast_dynamic-update-slice_fusion.2
  397.3 0.5 fusion.58
  397.8 1.4 bitcast_dynamic-update-slice_fusion.2
  399.2 39.3 %custom-call.33 = f32[4,128,128]{1,2,0:T(8,128)S(1)} custom-call(f32[4,128,128]{2,1,0:T(8,128)S(1)} %get-tuple-element.11), custom_call_target="InvertDiagBlocksLowerTriangular" | custom-call | tf_op jit(solution)/shard_map/triangular_solve | solution.py:91
  438.5 2.5 fusion.19
  441.0 3.1 convolution_subtract_fusion.1
  444.1 1.1 fusion.32
  445.2 4.6 convolution_subtract_fusion
  449.8 1.1 fusion.31
  450.9 7.2 fusion.8
  458.2 1.1 fusion.30
  459.3 27.9 %fusion = f32[1024,512]{1,0:T(8,128)} fusion(bf16[2048,1024]{1,0:T(8,128)(2,1)S(1)} %copy-done.8, bf16[2048,1024]{1,0:T(8,128)(2,1)S(1)} %copy-done.9, f32[2048,128]{0,1:T(8,128)S(1)} %fusion.30, f32[2048,128]{0,1:T(8,128)S(1)} %fusion.31, f32[2048,128]{0,1:T(8,128)S(1)} %fusion.32, f32[2048,128]{0,1:T(8,128)S(1)} %fusion.19), kind=kOutput, calls=%fused_computation.5 | convolution fusion | flops 12894339072 | bytes 14680064 | tf_op jit(solution)/shard_map/dot_general | solution.py:69
  487.2 6.2 all-to-all-start
  493.4 2.9 pad_maximum_fusion
  496.3 20.1 %all-to-all-done = f32[8,128,512]{2,1,0:T(8,128)} async-done(((f32[8,128,512]{2,1,0:T(8,128)}), f32[8,128,512]{2,1,0:T(8,128)}, u32[]{:S(2)}, u32[]{:S(2)}) %all-to-all-start) | async-done | bytes 2097184 | tf_op jit(solution)/shard_map/all_to_all | solution.py:25
  516.3 1.8 reduce_sum.27
  518.2 1.6 broadcast_in_dim.6
  519.7 5.7 all-to-all-start.1
  525.5 2.4 fusion.18
  527.9 2.3 copy.14
  530.3 21.2 %psum.59 = f32[512]{0:T(512)S(1)} all-reduce(f32[512]{0:T(512)S(1)} %multiply_reduce_fusion), channel_id=1, replica_groups=mesh['row_0'=4,'row_1'=2,'col_0'=4,'col_1'=2,'col_2'=2] {'row_0'}, use_global_device_ids=true, to_apply=%region_13.14 | all-reduce | flops 512 | bytes 4096 | tf_op jit(solution)/shard_map/psum | solution.py:30
  551.4 5.4 psum.60
  556.8 8.7 %psum.61 = f32[512]{0:T(512)S(1)} all-reduce(f32[512]{0:T(512)S(1)} %psum.60), channel_id=1, replica_groups=mesh['row_0'=4,'row_1'=2,'col_0'=4,'col_1'=2,'col_2'=2] {'col_0'}, use_global_device_ids=true, to_apply=%region_15.16 | all-reduce | flops 512 | bytes 4096 | tf_op jit(solution)/shard_map/psum | solution.py:30
  565.5 6.4 psum.62
  571.9 2.4 psum.63
  574.4 1.4 fusion.17
  575.9 1.7 copy.15
  577.6 1.6 broadcast_multiply_fusion
  579.2 106.5 %all-gather.5.cloned.1.call-done = bf16[16,1024,512]{2,1,0:T(8,128)(2,1)} async-done(((bf16[1,1024,512]{2,1,0:T(8,128)(2,1)}), bf16[16,1024,512]{2,1,0:T(8,128)(2,1)}) %all-gather.5.cloned.1.call-update) | async-done | bytes 16777232 | tf_op jit(solution)/shard_map/all_gather | solution.py:65
  685.7 1.7 dynamic-slice_bitcast_fusion.1
  687.3 39.4 %all-gather.3.cloned.1.call-done = bf16[1024,512]{0,1:T(8,128)(2,1)} async-done(((bf16[128,512]{0,1:T(8,128)(2,1)}), bf16[1024,512]{0,1:T(8,128)(2,1)}) %all-gather.3.cloned.1.call-update) | async-done | bytes 1048592 | tf_op jit(solution)/shard_map/all_gather | solution.py:61
  726.7 5.0 subtract_convert_fusion
  731.7 2.4 fusion.44
  734.1 8.6 %all-to-all-start.2 = ((f32[8,32,1024]{2,1,0:T(8,128)}), f32[8,32,1024]{2,1,0:T(8,128)}, u32[]{:S(2)}, u32[]{:S(2)}) async-start(f32[8,32,1024]{2,1,0:T(8,128)} %bitcast.17), calls=%async_computation.2 | async-start | bytes 2097152 | tf_op jit(solution)/shard_map/all_to_all | solution.py:25
  742.7 31.3 %subtract_convert_fusion.1 = bf16[2048,1024]{1,0:T(8,128)(2,1)} fusion(bf16[2048,1024]{1,0:T(8,128)(2,1)} %param.6, bf16[2048,1024]{1,0:T(8,128)(2,1)} %param.5, f32[1024,512]{1,0:T(8,128)} %bitcast.72, f32[2048,128]{0,1:T(8,128)} %copy-done.6, f32[2048,128]{0,1:T(8,128)} %copy-done.5, f32[2048,128]{0,1:T(8,128)} %copy-done.4, f32[2048,128]{0,1:T(8,128)S(1)} %fusion.19), kind=kOutput, calls=%fused_computation.3 | convolution fusion | flops 12900630528 | bytes 18874368 | tf_op jit(solution)/shard_map/dot_general | solution.py:75
  774.1 1.9 reduce_sum.29
  (58 shorter events, 1.8 us)
Async XLA Ops:
  7.2 1.6 copy-start
  7.2 113.0 %all-reduce.5.cloned.1.call-start = ((), (), s32[]{:S(2)}) async-start(), calls=%async_computation.4 | async-start | bytes 8388608 | tf_op jit(solution)/shard_map/psum | solution.py:83
  26.1 190.8 %all-reduce.7.cloned.1.call-start = ((), (), s32[]{:S(2)}) async-start(), calls=%async_computation.5 | async-start | bytes 8388608 | tf_op jit(solution)/shard_map/psum | solution.py:83
  120.2 184.2 %all-reduce.9.cloned.1.call-start = ((), (), s32[]{:S(2)}) async-start(), calls=%async_computation.6 | async-start | bytes 2097152 | tf_op jit(solution)/shard_map/psum | solution.py:89
  399.2 39.3 %copy-start.7 = (f32[512,512]{1,0:T(8,128)}, f32[512,512]{1,0:T(8,128)S(1)}, u32[]{:S(2)}) copy-start(f32[512,512]{1,0:T(8,128)S(1)} %get-tuple-element.104) | copy-start | bytes 3145732
  438.5 6.6 copy-start.2
  445.2 48.2 %copy-start.4 = (f32[2048,128]{0,1:T(8,128)}, f32[2048,128]{0,1:T(8,128)S(1)}, u32[]{:S(2)}) copy-start(f32[2048,128]{0,1:T(8,128)S(1)} %fusion.32) | copy-start | bytes 3145732
  449.8 9.5 %copy-start.9 = (bf16[2048,1024]{1,0:T(8,128)(2,1)S(1)}, bf16[2048,1024]{1,0:T(8,128)(2,1)}, u32[]{:S(2)}) copy-start(bf16[2048,1024]{1,0:T(8,128)(2,1)} %param.5) | copy-start | bytes 12582916
  450.9 42.5 %copy-start.5 = (f32[2048,128]{0,1:T(8,128)}, f32[2048,128]{0,1:T(8,128)S(1)}, u32[]{:S(2)}) copy-start(f32[2048,128]{0,1:T(8,128)S(1)} %fusion.31) | copy-start | bytes 3145732
  450.9 8.4 %copy-start.8 = (bf16[2048,1024]{1,0:T(8,128)(2,1)S(1)}, bf16[2048,1024]{1,0:T(8,128)(2,1)}, u32[]{:S(2)}) copy-start(bf16[2048,1024]{1,0:T(8,128)(2,1)} %param.6) | copy-start | bytes 12582916
  459.3 27.9 %copy-start.6 = (f32[2048,128]{0,1:T(8,128)}, f32[2048,128]{0,1:T(8,128)S(1)}, u32[]{:S(2)}) copy-start(f32[2048,128]{0,1:T(8,128)S(1)} %fusion.30) | copy-start | bytes 3145732
  487.2 29.1 %all-to-all-start = ((f32[8,128,512]{2,1,0:T(8,128)}), f32[8,128,512]{2,1,0:T(8,128)}, u32[]{:S(2)}, u32[]{:S(2)}) async-start(f32[8,128,512]{2,1,0:T(8,128)} %bitcast.73), calls=%async_computation | async-start | bytes 4194304 | tf_op jit(solution)/shard_map/all_to_all | solution.py:25
  519.7 54.6 %all-to-all-start.1 = ((f32[8,128,512]{2,1,0:T(8,128)}), f32[8,128,512]{2,1,0:T(8,128)S(1)}, u32[]{:S(2)}, u32[]{:S(2)}) async-start(f32[8,128,512]{2,1,0:T(8,128)} %broadcast_in_dim.6), calls=%async_computation.1 | async-start | bytes 4194304 | tf_op jit(solution)/shard_map/all_to_all | solution.py:41
  525.5 50.4 %reduce-scatter.4.cloned.1.call-start = ((), (), s32[]{:S(2)}) async-start(), calls=%async_computation.9 | async-start | bytes 1179648
  530.2 155.5 %all-gather.5.cloned.1.call-start = ((), (), s32[]{:S(2)}) async-start(), calls=%async_computation.8 | async-start | bytes 17825792 | tf_op jit(solution)/shard_map/all_gather | solution.py:65
  574.4 4.8 copy-start.3
  575.8 150.9 %all-gather.3.cloned.1.call-start = ((), (), s32[]{:S(2)}) async-start(), calls=%async_computation.7 | async-start | bytes 1179648 | tf_op jit(solution)/shard_map/all_gather | solution.py:61
  726.7 5.0 copy-start.10
  731.7 2.4 copy-start.11
  734.1 39.9 %all-to-all-start.2 = ((f32[8,32,1024]{2,1,0:T(8,128)}), f32[8,32,1024]{2,1,0:T(8,128)}, u32[]{:S(2)}, u32[]{:S(2)}) async-start(f32[8,32,1024]{2,1,0:T(8,128)} %bitcast.17), calls=%async_computation.2 | async-start | bytes 2097152 | tf_op jit(solution)/shard_map/all_to_all | solution.py:25
  742.7 33.3 %copy-start.1 = (f32[1024,512]{1,0:T(8,128)S(1)}, f32[1024,512]{1,0:T(8,128)}, u32[]{:S(2)}) copy-start(f32[1024,512]{1,0:T(8,128)} %param.7) | copy-start | bytes 6291460
Sparse Core Ops, SparseCore 0:
  26.2 93.9 all-reduce.4
  122.9 93.9 all-reduce.6
  228.6 75.7 all-reduce.8
  530.3 43.7 reduce-scatter.3
  576.9 108.7 all-gather.4
  687.7 38.9 all-gather.2
